TPU v7x, 32 devices: a whole 2x2x4 slice. The times are simulated.
32 devices in a mesh: fsdp: 8 (over z, y), tp: 4 (over x, core).
Axes of the slice: x: 2, y: 2, z: 4, core: 2. Of those that a mesh axis runs over, the one named last changes fastest.
Arguments:
- inputs: bfloat16 [16, 736, 1152], P('fsdp', 'tp'), may hold values from -6 to 6
- cotangent: bfloat16 [16, 736, 1152], P('fsdp', 'tp'), may hold values from -6 to 6
- lengths: int32 [16], P('fsdp'), may hold values from 1 to 729, as said below
- ln1_gain: bfloat16 [1152], P('fsdp'), may hold values from 0.099609375 to 1.8984375
- ln1_bias: bfloat16 [1152], P('fsdp'), may hold values from -0.3125 to 0.3125
- q_weight: bfloat16 [1152, 1152], P('fsdp', 'tp'), may hold values from -0.1875 to 0.1875
- q_bias: bfloat16 [1152], P('tp'), may hold values from -3 to 3
- k_weight: bfloat16 [1152, 1152], P('fsdp', 'tp'), may hold values from -0.1875 to 0.1875
- v_weight: bfloat16 [1152, 1152], P('fsdp', 'tp'), may hold values from -0.1875 to 0.1875
- v_bias: bfloat16 [1152], P('tp'), may hold values from -0.1875 to 0.1875
- out_weight: bfloat16 [1152, 1152], P('tp', 'fsdp'), may hold values from -2.5 to 2.5
- out_bias: bfloat16 [1152], P('fsdp'), may hold values from -1.75 to 1.75
- ln2_gain: bfloat16 [1152], P('fsdp'), may hold values from 0.099609375 to 1.8984375
- ln2_bias: bfloat16 [1152], P('fsdp'), may hold values from -1.75 to 1.75
- up_weight: bfloat16 [1152, 4304], P('fsdp', 'tp'), may hold values from -0.1875 to 0.1875
- up_bias: bfloat16 [4304], P('tp'), may hold values from -1.75 to 1.75
- down_weight: bfloat16 [4304, 1152], P('tp', 'fsdp'), may hold values from -0.09375 to 0.09375
- down_bias: bfloat16 [1152], P('fsdp'), may hold values from -1.75 to 1.75
Outputs:
- layer_out: bfloat16 [16, 736, 1152], P('fsdp', 'tp')
- input_grad: float32 [16, 736, 1152], P('fsdp', 'tp')
- ln1_gain_grad: float32 [1152], P('fsdp')
- ln1_bias_grad: float32 [1152], P('fsdp')
- q_weight_grad: float32 [1152, 1152], P('fsdp', 'tp')
- q_bias_grad: float32 [1152], P('tp')
- k_weight_grad: float32 [1152, 1152], P('fsdp', 'tp')
- v_weight_grad: float32 [1152, 1152], P('fsdp', 'tp')
- v_bias_grad: float32 [1152], P('tp')
- out_weight_grad: float32 [1152, 1152], P('tp', 'fsdp')
- out_bias_grad: float32 [1152], P('fsdp')
- ln2_gain_grad: float32 [1152], P('fsdp')
- ln2_bias_grad: float32 [1152], P('fsdp')
- up_weight_grad: float32 [1152, 4304], P('fsdp', 'tp')
- up_bias_grad: float32 [4304], P('tp')
- down_weight_grad: float32 [4304, 1152], P('tp', 'fsdp')
- down_bias_grad: float32 [1152], P('fsdp')
Inputs may be any that keep to these rules, and one draw needn't show every extreme that they name: `lengths`: each slot either holds one image of 729 tokens or is empty with length 1; exactly 11 slots hold images, which ones drawn from the seed.
All inputs are finite; a program needn't handle non-finite values.
Results may differ from a plain program's by a relative error of at most 0.013.
Values may be sent and summed in bfloat16 or wider, within the bound.
No kernel may reach another device: no remote copies, remote signals or barrier semaphores. Data moves between devices by JAX's collectives and lax.ppermute only.
A program may use at most 192 MiB of HBM per device.

v0:
```python
import jax
import jax.numpy as jnp
from jax import lax
from jax.sharding import PartitionSpec as P

HD = 72
epsilon = 1e-06
negative_big = -1e30


def layer_norm(row_block, gain_vec, shift_vec):
    average = jnp.mean(row_block, -1, keepdims=True)
    center = row_block - average
    variance = jnp.mean(center * center, -1, keepdims=True)
    return center * lax.rsqrt(variance + epsilon) * gain_vec + shift_vec


def gelu_tanh(values_in):
    return jax.nn.gelu(values_in, approximate=True)


def plain_dot(left, right):
    return jnp.dot(left, right, preferred_element_type=jnp.float32)


def contract_rows(left, right):
    return lax.dot_general(
        left, right, (((0,), (0,)), ((), ())), preferred_element_type=jnp.float32
    )


def contract_cols(left, right):
    return lax.dot_general(
        left, right, (((1,), (1,)), ((), ())), preferred_element_type=jnp.float32
    )


def local(
    inputs,
    cotangent,
    lengths,
    ln1_gain,
    ln1_bias,
    q_weight,
    q_bias,
    k_weight,
    v_weight,
    v_bias,
    out_weight,
    out_bias,
    ln2_gain,
    ln2_bias,
    up_weight,
    up_bias,
    down_weight,
    down_bias,
):
    tp_count = lax.axis_size("tp")
    tp_index = lax.axis_index("tp")
    fsdp_index = lax.axis_index("fsdp")
    micro_count = inputs.shape[0]
    local_rows = inputs.shape[1]
    model_width = inputs.shape[2]
    seq_len = local_rows * tp_count
    head_width = q_weight.shape[1]
    heads_here = head_width // HD
    unit_width = up_weight.shape[1]
    scale_value = HD ** (-0.5)
    q_shift = q_bias.astype(jnp.float32)
    v_shift = v_bias.astype(jnp.float32)
    up_shift = up_bias.astype(jnp.float32)

    def fetch_weights():
        attn_full = (
            lax.all_gather(ln1_gain, "fsdp", axis=0, tiled=True),
            lax.all_gather(ln1_bias, "fsdp", axis=0, tiled=True),
            lax.all_gather(q_weight, "fsdp", axis=0, tiled=True),
            lax.all_gather(k_weight, "fsdp", axis=0, tiled=True),
            lax.all_gather(v_weight, "fsdp", axis=0, tiled=True),
            lax.all_gather(out_weight, "fsdp", axis=1, tiled=True),
            lax.all_gather(out_bias, "fsdp", axis=0, tiled=True),
        )
        mlp_full = (
            lax.all_gather(ln2_gain, "fsdp", axis=0, tiled=True),
            lax.all_gather(ln2_bias, "fsdp", axis=0, tiled=True),
            lax.all_gather(up_weight, "fsdp", axis=0, tiled=True),
            lax.all_gather(down_weight, "fsdp", axis=1, tiled=True),
            lax.all_gather(down_bias, "fsdp", axis=0, tiled=True),
        )
        return (attn_full, mlp_full)

    def masked_scores(queries, keys_all, key_valid):
        query_heads = queries.reshape(seq_len, heads_here, HD)
        key_heads = keys_all.reshape(seq_len, heads_here, HD)
        scores = (
            jnp.einsum("qhd,khd->hqk", query_heads, key_heads, preferred_element_type=jnp.float32)
            * scale_value
        )
        return jnp.where(key_valid[None, None, :], scores, negative_big)

    def forward(slot_rows, length, attn_full, mlp_full):
        gain_one, shift_one, wq_full, wk_full, wv_full, wo_full, bo_full = attn_full
        gain_two, shift_two, w_up, w_down, bd_full = mlp_full
        key_valid = jnp.arange(seq_len, dtype=jnp.int32) < length
        norm_one = layer_norm(
            slot_rows, gain_one.astype(jnp.float32), shift_one.astype(jnp.float32)
        ).astype(jnp.bfloat16)
        norm_full = lax.all_gather(norm_one, "tp", axis=0, tiled=True)
        queries = (plain_dot(norm_full, wq_full) + q_shift).astype(jnp.bfloat16)
        keys_all = plain_dot(norm_full, wk_full).astype(jnp.bfloat16)
        values_all = (plain_dot(norm_full, wv_full) + v_shift).astype(jnp.bfloat16)
        scores = masked_scores(queries, keys_all, key_valid)
        row_max = jnp.max(scores, -1, keepdims=True)
        row_total = jnp.sum(jnp.exp(scores - row_max), -1, keepdims=True)
        log_total = row_max + jnp.log(row_total)
        soft_low = jnp.exp(scores - log_total).astype(jnp.bfloat16)
        value_heads = values_all.reshape(seq_len, heads_here, HD)
        mixed_heads = jnp.einsum(
            "hqk,khd->qhd", soft_low, value_heads, preferred_element_type=jnp.float32
        )
        mixed_heads = mixed_heads.astype(jnp.bfloat16).reshape(seq_len, head_width)
        attended = lax.psum_scatter(
            plain_dot(mixed_heads, wo_full), "tp", scatter_dimension=0, tiled=True
        )
        middle = slot_rows + attended + bo_full.astype(jnp.float32)
        norm_two = layer_norm(
            middle, gain_two.astype(jnp.float32), shift_two.astype(jnp.float32)
        ).astype(jnp.bfloat16)
        norm_two_full = lax.all_gather(norm_two, "tp", axis=0, tiled=True)
        hidden = plain_dot(norm_two_full, w_up) + up_shift
        active = gelu_tanh(hidden).astype(jnp.bfloat16)
        mlp_rows = lax.psum_scatter(
            plain_dot(active, w_down), "tp", scatter_dimension=0, tiled=True
        )
        out_rows = middle + mlp_rows + bd_full.astype(jnp.float32)
        kept_state = (
            norm_full,
            queries,
            keys_all,
            values_all,
            log_total,
            mixed_heads,
            middle,
            norm_two_full,
            hidden,
            active,
        )
        return (out_rows, kept_state)

    outputs = []
    for slot_index in range(micro_count):
        attn_full, mlp_full = fetch_weights()
        out_rows, kept_state = forward(
            inputs[slot_index].astype(jnp.float32), lengths[slot_index], attn_full, mlp_full
        )
        outputs.append(out_rows.astype(jnp.bfloat16))
    grad_list = []
    totals = None
    for slot_index in range(micro_count):
        attn_full, mlp_full = fetch_weights()
        slot_rows = inputs[slot_index].astype(jnp.float32)
        kept_state = forward(slot_rows, lengths[slot_index], attn_full, mlp_full)[1]
        backward_length = lengths[slot_index]
        (
            backward_gain_one,
            backward_shift_one,
            backward_wq_full,
            backward_wk_full,
            backward_wv_full,
            backward_wo_full,
            backward_bo_full,
        ) = attn_full
        backward_gain_two, backward_shift_two, backward_w_up, backward_w_down, backward_bd_full = (
            mlp_full
        )
        (
            backward_norm_full,
            backward_queries,
            backward_keys_all,
            backward_values_all,
            backward_log_total,
            backward_mixed_heads,
            backward_middle,
            backward_norm_two_full,
            backward_hidden,
            backward_active,
        ) = kept_state
        backward_key_valid = jnp.arange(seq_len, dtype=jnp.int32) < backward_length
        row_valid = (
            jnp.arange(local_rows, dtype=jnp.int32) + tp_index * local_rows < backward_length
        ).astype(jnp.float32)
        grad_out = cotangent[slot_index].astype(jnp.float32) * row_valid[:, None]
        backward_down_sum = jnp.sum(grad_out, 0)
        grad_out_full = lax.all_gather(grad_out.astype(jnp.bfloat16), "tp", axis=0, tiled=True)
        backward_grad_w_down = contract_rows(backward_active, grad_out_full)
        grad_active = contract_cols(grad_out_full, backward_w_down)
        gelu_pull = jax.vjp(gelu_tanh, backward_hidden)[1]
        grad_hidden = gelu_pull(grad_active)[0].astype(jnp.bfloat16)
        backward_up_sum = jnp.sum(grad_hidden.astype(jnp.float32), 0)
        backward_grad_w_up = contract_rows(backward_norm_two_full, grad_hidden)
        grad_norm_two = lax.psum_scatter(
            contract_cols(grad_hidden, backward_w_up), "tp", scatter_dimension=0, tiled=True
        )
        norm_two_pull = jax.vjp(
            layer_norm,
            backward_middle,
            backward_gain_two.astype(jnp.float32),
            backward_shift_two.astype(jnp.float32),
        )[1]
        middle_part, backward_gain_two_grad, backward_shift_two_grad = norm_two_pull(grad_norm_two)
        grad_middle = grad_out + middle_part
        backward_out_sum = jnp.sum(grad_middle, 0)
        grad_middle_full = lax.all_gather(
            grad_middle.astype(jnp.bfloat16), "tp", axis=0, tiled=True
        )
        backward_grad_w_out = contract_rows(backward_mixed_heads, grad_middle_full)
        grad_mixed = (
            contract_cols(grad_middle_full, backward_wo_full)
            .astype(jnp.bfloat16)
            .reshape(seq_len, heads_here, HD)
        )
        soft_weights = jnp.exp(
            masked_scores(backward_queries, backward_keys_all, backward_key_valid)
            - backward_log_total
        )
        backward_soft_low = soft_weights.astype(jnp.bfloat16)
        backward_query_heads = backward_queries.reshape(seq_len, heads_here, HD)
        backward_key_heads = backward_keys_all.reshape(seq_len, heads_here, HD)
        backward_value_heads = backward_values_all.reshape(seq_len, heads_here, HD)
        grad_soft = jnp.einsum(
            "qhd,khd->hqk", grad_mixed, backward_value_heads, preferred_element_type=jnp.float32
        )
        row_inner = jnp.sum(soft_weights * grad_soft, -1, keepdims=True)
        grad_scores = (soft_weights * (grad_soft - row_inner)).astype(jnp.bfloat16)
        grad_queries = (
            (
                jnp.einsum(
                    "hqk,khd->qhd",
                    grad_scores,
                    backward_key_heads,
                    preferred_element_type=jnp.float32,
                )
                * scale_value
            )
            .astype(jnp.bfloat16)
            .reshape(seq_len, head_width)
        )
        grad_keys = (
            (
                jnp.einsum(
                    "hqk,qhd->khd",
                    grad_scores,
                    backward_query_heads,
                    preferred_element_type=jnp.float32,
                )
                * scale_value
            )
            .astype(jnp.bfloat16)
            .reshape(seq_len, head_width)
        )
        grad_values = (
            jnp.einsum(
                "hqk,qhd->khd", backward_soft_low, grad_mixed, preferred_element_type=jnp.float32
            )
            .astype(jnp.bfloat16)
            .reshape(seq_len, head_width)
        )
        backward_query_sum = jnp.sum(grad_queries.astype(jnp.float32), 0)
        backward_value_sum = jnp.sum(grad_values.astype(jnp.float32), 0)
        backward_grad_wq = contract_rows(backward_norm_full, grad_queries)
        backward_grad_wk = contract_rows(backward_norm_full, grad_keys)
        backward_grad_wv = contract_rows(backward_norm_full, grad_values)
        part_q = contract_cols(grad_queries, backward_wq_full)
        part_k = contract_cols(grad_keys, backward_wk_full)
        part_v = contract_cols(grad_values, backward_wv_full)
        grad_norm_one = lax.psum_scatter(
            part_q + part_k + part_v, "tp", scatter_dimension=0, tiled=True
        )
        norm_one_pull = jax.vjp(
            layer_norm,
            slot_rows,
            backward_gain_one.astype(jnp.float32),
            backward_shift_one.astype(jnp.float32),
        )[1]
        rows_part, backward_gain_one_grad, backward_shift_one_grad = norm_one_pull(grad_norm_one)
        grad_rows = grad_middle + rows_part
        slot_grads = (
            backward_gain_one_grad,
            backward_shift_one_grad,
            backward_grad_wq,
            backward_query_sum,
            backward_grad_wk,
            backward_grad_wv,
            backward_value_sum,
            backward_grad_w_out,
            backward_out_sum,
            backward_gain_two_grad,
            backward_shift_two_grad,
            backward_grad_w_up,
            backward_up_sum,
            backward_grad_w_down,
            backward_down_sum,
        )
        grad_rows, slot_grads = (grad_rows, slot_grads)
        grad_list.append(grad_rows)
        if totals is None:
            totals = slot_grads
        else:
            totals = jax.tree.map(jnp.add, totals, slot_grads)
    (
        gain_one_grad,
        shift_one_grad,
        grad_wq,
        query_sum,
        grad_wk,
        grad_wv,
        value_sum,
        grad_w_out,
        out_sum,
        gain_two_grad,
        shift_two_grad,
        grad_w_up,
        up_sum,
        grad_w_down,
        down_sum,
    ) = totals
    summed_weights = (
        lax.psum_scatter(grad_wq, "fsdp", scatter_dimension=0, tiled=True),
        lax.psum_scatter(grad_wk, "fsdp", scatter_dimension=0, tiled=True),
        lax.psum_scatter(grad_wv, "fsdp", scatter_dimension=0, tiled=True),
        lax.psum_scatter(grad_w_out, "fsdp", scatter_dimension=1, tiled=True),
        lax.psum_scatter(grad_w_up, "fsdp", scatter_dimension=0, tiled=True),
        lax.psum_scatter(grad_w_down, "fsdp", scatter_dimension=1, tiled=True),
    )
    width_stack = jnp.stack(
        [gain_one_grad, shift_one_grad, out_sum, gain_two_grad, shift_two_grad, down_sum], 0
    )
    head_stack = jnp.zeros((2, head_width * tp_count), jnp.float32)
    head_stack = lax.dynamic_update_slice_in_dim(
        head_stack, jnp.stack([query_sum, value_sum], 0), tp_index * head_width, 1
    )
    unit_line = jnp.zeros((unit_width * tp_count,), jnp.float32)
    unit_line = lax.dynamic_update_slice_in_dim(unit_line, up_sum, tp_index * unit_width, 0)
    summed_small = lax.psum((width_stack, head_stack, unit_line), ("fsdp", "tp"))
    shard_size = model_width // lax.axis_size("fsdp")
    width_pieces = lax.dynamic_slice_in_dim(summed_small[0], fsdp_index * shard_size, shard_size, 1)
    head_pieces = lax.dynamic_slice_in_dim(summed_small[1], tp_index * head_width, head_width, 1)
    unit_piece = lax.dynamic_slice_in_dim(summed_small[2], tp_index * unit_width, unit_width, 0)
    return (
        jnp.stack(outputs, 0),
        jnp.stack(grad_list, 0),
        width_pieces[0],
        width_pieces[1],
        summed_weights[0],
        head_pieces[0],
        summed_weights[1],
        summed_weights[2],
        head_pieces[1],
        summed_weights[3],
        width_pieces[2],
        width_pieces[3],
        width_pieces[4],
        summed_weights[4],
        unit_piece,
        summed_weights[5],
        width_pieces[5],
    )


def solution(mesh):
    in_specs = (
        P("fsdp", "tp", None),
        P("fsdp", "tp", None),
        P("fsdp"),
        P("fsdp"),
        P("fsdp"),
        P("fsdp", "tp"),
        P("tp"),
        P("fsdp", "tp"),
        P("fsdp", "tp"),
        P("tp"),
        P("tp", "fsdp"),
        P("fsdp"),
        P("fsdp"),
        P("fsdp"),
        P("fsdp", "tp"),
        P("tp"),
        P("tp", "fsdp"),
        P("fsdp"),
    )
    out_specs = (
        P("fsdp", "tp", None),
        P("fsdp", "tp", None),
        P("fsdp"),
        P("fsdp"),
        P("fsdp", "tp"),
        P("tp"),
        P("fsdp", "tp"),
        P("fsdp", "tp"),
        P("tp"),
        P("tp", "fsdp"),
        P("fsdp"),
        P("fsdp"),
        P("fsdp"),
        P("fsdp", "tp"),
        P("tp"),
        P("tp", "fsdp"),
        P("fsdp"),
    )
    return jax.shard_map(local, mesh=mesh, in_specs=in_specs, out_specs=out_specs, check_vma=False)
```

profile of v0, /device:TPU:0, one launch (start us, length us, event | category | flops | bytes accessed | tf_op | source)
XLA Modules:
  0.0 1294.0 jit_solution(5558494795576318744)
XLA Ops:
  14.4 38.8 %all-reduce.15 = (bf16[1152]{0:T(1024)(128)(2,1)S(1)}, bf16[1152]{0:T(1024)(128)(2,1)S(1)}, bf16[1152]{0:T(1024)(128)(2,1)S(1)}, bf16[1152]{0:T(1024)(128)(2,1)S...) all-reduce(bf16[1152]{0:T(1024)(128)(2,1)S(1)} %dynamic-update-slic, ...), channel_id=1, replica_groups=mesh['fsdp'=8,'tp'=4] {'fsdp'}, use_global_device_ids=true, to_apply=%add.1 | all-reduce | flops 6912 | bytes 27648
  56.7 2.4 fusion.46
  60.0 32.5 %all_gather.44 = bf16[1152,288]{1,0:T(8,128)(2,1)S(1)} all-gather(bf16[144,288]{1,0:T(8,128)(2,1)S(1)} %copy-done.54), channel_id=1, replica_groups=mesh['fsdp'=8,'tp'=4] {'fsdp'}, dimensions={0}, use_global_device_ids=true | all-gather | bytes 746496 | tf_op jit(solution)/shard_map/all_gather | solution.py:77
  92.5 32.2 %all_gather.45 = bf16[1152,288]{1,0:T(8,128)(2,1)S(1)} all-gather(bf16[144,288]{1,0:T(8,128)(2,1)S(1)} %copy-done.55), channel_id=1, replica_groups=mesh['fsdp'=8,'tp'=4] {'fsdp'}, dimensions={0}, use_global_device_ids=true | all-gather | bytes 746496 | tf_op jit(solution)/shard_map/all_gather | solution.py:78
  126.1 34.5 %all_gather.43 = bf16[1152,288]{1,0:T(8,128)(2,1)} all-gather(bf16[144,288]{1,0:T(8,128)(2,1)S(1)} %copy-done.56), channel_id=1, replica_groups=mesh['fsdp'=8,'tp'=4] {'fsdp'}, dimensions={0}, use_global_device_ids=true | all-gather | bytes 746496 | tf_op jit(solution)/shard_map/all_gather | solution.py:79
  160.6 32.0 %all_gather.46 = bf16[288,1152]{0,1:T(8,128)(2,1)S(1)} all-gather(bf16[288,144]{0,1:T(8,128)(2,1)S(1)} %copy-done.57), channel_id=1, replica_groups=mesh['fsdp'=8,'tp'=4] {'fsdp'}, dimensions={1}, use_global_device_ids=true | all-gather | bytes 746496 | tf_op jit(solution)/shard_map/all_gather | solution.py:80
  192.6 2.6 convolution_convert_fusion.6
  198.2 2.3 exponential_reduce_fusion
  206.9 3.0 fusion.86
  210.9 2.4 convolution_convert_fusion.7
  216.2 2.3 exponential_reduce_fusion.1
  225.0 2.8 fusion.85
  231.9 15.0 %reduce-scatter.47.cloned.1.call-done = f32[184,1152]{1,0:T(8,128)} async-done(((f32[736,1152]{1,0:T(8,128)}), f32[184,1152]{1,0:T(8,128)}) %reduce-scatter.47.cloned.1.call-update) | async-done | bytes 847888
  247.0 42.0 %reduce-scatter.43.cloned.1.call-done = f32[184,1152]{1,0:T(8,128)} async-done(((f32[736,1152]{1,0:T(8,128)}), f32[184,1152]{1,0:T(8,128)}) %reduce-scatter.43.cloned.1.call-update) | async-done | bytes 847888
  294.4 17.0 %all-gather.23.cloned.1.call-done = bf16[736,1152]{1,0:T(8,128)(2,1)} async-done(((bf16[184,1152]{1,0:T(8,128)(2,1)}), bf16[736,1152]{1,0:T(8,128)(2,1)}) %all-gather.23.cloned.1.call-update) | async-done | bytes 1695760 | tf_op jit(solution)/shard_map/all_gather | solution.py:194
  311.4 57.1 %all-gather.17.cloned.1.call-done = bf16[1076,1152]{0,1:T(8,128)(2,1)} async-done(((bf16[1076,144]{0,1:T(8,128)(2,1)}), bf16[1076,1152]{0,1:T(8,128)(2,1)}) %all-gather.17.cloned.1.call-update) | async-done | bytes 2479120 | tf_op jit(solution)/shard_map/all_gather | solution.py:87
  368.5 6.4 fusion.87
  374.9 49.4 %all-gather.15.cloned.1.call-done = bf16[1152,1076]{1,0:T(8,128)(2,1)} async-done(((bf16[144,1076]{1,0:T(8,128)(2,1)}), bf16[1152,1076]{1,0:T(8,128)(2,1)}) %all-gather.15.cloned.1.call-update) | async-done | bytes 2479120 | tf_op jit(solution)/shard_map/all_gather | solution.py:86
  424.3 20.5 %all-gather.13.cloned.1.call-done = bf16[736,1152]{1,0:T(8,128)(2,1)} async-done(((bf16[184,1152]{1,0:T(8,128)(2,1)}), bf16[736,1152]{1,0:T(8,128)(2,1)}) %all-gather.13.cloned.1.call-update) | async-done | bytes 1695760 | tf_op jit(solution)/shard_map/all_gather | solution.py:129
  444.8 10.3 convert_reduce_fusion.1
  456.2 4.5 fusion.88
  461.0 5.7 all-gather.27.cloned.1.call-done
  466.7 6.4 fusion.90
  473.1 15.4 %all-gather.21.cloned.1.call-done = bf16[736,1152]{1,0:T(8,128)(2,1)} async-done(((bf16[184,1152]{1,0:T(8,128)(2,1)}), bf16[736,1152]{1,0:T(8,128)(2,1)}) %all-gather.21.cloned.1.call-update) | async-done | bytes 1695760 | tf_op jit(solution)/shard_map/all_gather | solution.py:129
  488.5 10.2 convert_reduce_fusion
  499.9 4.4 fusion.91
  504.6 7.8 fusion.73
  512.5 7.6 fusion.74
  520.2 10.4 reduce-scatter.51.cloned.1.call-done
  530.6 42.1 %reduce-scatter.55.cloned.1.call-done = f32[184,1152]{1,0:T(8,128)} async-done(((f32[736,1152]{1,0:T(8,128)}), f32[184,1152]{1,0:T(8,128)}) %reduce-scatter.55.cloned.1.call-update) | async-done | bytes 847888
  574.8 39.9 %reduce-scatter.45.cloned.1.call-done = f32[184,1152]{1,0:T(8,128)} async-done(((f32[736,1152]{1,0:T(8,128)}), f32[184,1152]{1,0:T(8,128)}) %reduce-scatter.45.cloned.1.call-update) | async-done | bytes 847888
  614.7 42.1 %reduce-scatter.49.cloned.1.call-done = f32[184,1152]{1,0:T(8,128)} async-done(((f32[736,1152]{1,0:T(8,128)}), f32[184,1152]{1,0:T(8,128)}) %reduce-scatter.49.cloned.1.call-update) | async-done | bytes 847888
  656.8 3.6 fusion.78
  661.3 3.1 fusion.54
  665.4 19.5 %all-gather.29.cloned.1.call-done = bf16[736,1152]{1,0:T(8,128)(2,1)} async-done(((bf16[184,1152]{1,0:T(8,128)(2,1)}), bf16[736,1152]{1,0:T(8,128)(2,1)}) %all-gather.29.cloned.1.call-update) | async-done | bytes 1695760 | tf_op jit(solution)/shard_map/all_gather | solution.py:213
  684.9 2.2 convolution_convert_fusion.4
  687.2 6.1 multiply_reduce_fusion
  694.0 4.1 multiply_convert_fusion
  698.1 2.6 convert_reduce_fusion.6
  706.8 3.0 convolution_add_fusion.2
  713.2 6.6 multiply_reduce_fusion.1
  721.4 2.9 multiply_convert_fusion.1
  731.8 2.9 convolution_add_fusion.4
  736.2 4.2 fusion.97
  740.4 5.1 convolution_add_fusion.1
  746.9 4.7 fusion.72
  751.7 5.1 convolution_add_fusion
  757.9 2.6 fusion.96
  760.6 2.4 convolution_add_fusion.8
  763.1 2.7 fusion.95
  765.9 2.4 convolution_add_fusion.9
  768.4 2.6 fusion.94
  771.1 2.4 convolution_add_fusion.10
  776.8 2.7 fusion.93
  779.5 2.4 convolution_add_fusion.11
  782.2 9.3 reduce-scatter.53.cloned.1.call-done
  793.6 2.9 fusion.47
  796.5 43.7 %all-reduce.14 = (f32[6,1152]{1,0:T(8,128)}, f32[2,1152]{1,0:T(2,128)S(1)}, f32[4304]{0:T(1024)S(1)}) all-reduce(f32[6,1152]{1,0:T(8,128)S(1)} %stack.38, f32[2,1152]{1,0:T(2,128)S(1)} %dynamic_update_slice.6, f32[4304]{0:T(1024)S(1)} %add_dynamic-update-slice_fusion), channel_id=1, replica_groups=mesh['fsdp'=8,'tp'=4] {'fsdp','tp'}, use_global_device_ids=true, to_apply=%region_42.43 | all-reduce | flops 13520 | bytes 108160 | tf_op jit(solution)/shard_map/psum | solution.py:344
  848.7 52.2 %reduce-scatter.39.cloned.1.call-done = f32[144,1076]{1,0:T(8,128)} async-done(((f32[1152,1076]{1,0:T(8,128)}), f32[144,1076]{1,0:T(8,128)}) %reduce-scatter.39.cloned.1.call-update) | async-done | bytes 619792 | tf_op jit(solution)/shard_map/reduce_scatter | solution.py:332
  901.0 108.4 %reduce-scatter.41.cloned.1.call-done = f32[1076,144]{0,1:T(8,128)} async-done(((f32[1076,1152]{0,1:T(8,128)}), f32[1076,144]{0,1:T(8,128)}) %reduce-scatter.41.cloned.1.call-update) | async-done | bytes 619792 | tf_op jit(solution)/shard_map/reduce_scatter | solution.py:333
  1009.4 69.9 %reduce-scatter.37.cloned.1.call-done = f32[288,144]{0,1:T(8,128)} async-done(((f32[288,1152]{0,1:T(8,128)}), f32[288,144]{0,1:T(8,128)}) %reduce-scatter.37.cloned.1.call-update) | async-done | bytes 165904 | tf_op jit(solution)/shard_map/reduce_scatter | solution.py:331
  1079.3 69.5 %reduce-scatter.35.cloned.1.call-done = f32[144,288]{1,0:T(8,128)} async-done(((f32[1152,288]{1,0:T(8,128)}), f32[144,288]{1,0:T(8,128)}) %reduce-scatter.35.cloned.1.call-update) | async-done | bytes 165904 | tf_op jit(solution)/shard_map/reduce_scatter | solution.py:330
  1148.7 69.0 %reduce-scatter.33.cloned.1.call-done = f32[144,288]{1,0:T(8,128)} async-done(((f32[1152,288]{1,0:T(8,128)}), f32[144,288]{1,0:T(8,128)}) %reduce-scatter.33.cloned.1.call-update) | async-done | bytes 165904 | tf_op jit(solution)/shard_map/reduce_scatter | solution.py:329
  1217.7 69.0 %reduce-scatter.31.cloned.1.call-done = f32[144,288]{1,0:T(8,128)} async-done(((f32[1152,288]{1,0:T(8,128)}), f32[144,288]{1,0:T(8,128)}) %reduce-scatter.31.cloned.1.call-update) | async-done | bytes 165904 | tf_op jit(solution)/shard_map/reduce_scatter | solution.py:328
  (385 shorter events, 85.1 us)
Async XLA Ops:
  7.2 52.8 %copy-start.54 = (bf16[144,288]{1,0:T(8,128)(2,1)S(1)}, bf16[144,288]{1,0:T(8,128)(2,1)}, u32[]{:S(2)}) copy-start(bf16[144,288]{1,0:T(8,128)(2,1)} %param.23) | copy-start | bytes 248836
  7.2 85.3 %copy-start.91 = (bf16[288]{0:T(512)(128)(2,1)S(1)}, bf16[288]{0:T(512)(128)(2,1)}, u32[]{:S(2)}) copy-start(bf16[288]{0:T(512)(128)(2,1)} %param.24) | copy-start | bytes 1732
  7.2 85.3 %copy-start.55 = (bf16[144,288]{1,0:T(8,128)(2,1)S(1)}, bf16[144,288]{1,0:T(8,128)(2,1)}, u32[]{:S(2)}) copy-start(bf16[144,288]{1,0:T(8,128)(2,1)} %param.25) | copy-start | bytes 248836
  7.2 117.5 %copy-start.90 = (s32[2]{0:T(128)S(1)}, s32[2]{0:T(128)}, u32[]{:S(2)}) copy-start(s32[2]{0:T(128)} %param.20) | copy-start | bytes 28
  7.2 118.8 %copy-start.56 = (bf16[144,288]{1,0:T(8,128)(2,1)S(1)}, bf16[144,288]{1,0:T(8,128)(2,1)}, u32[]{:S(2)}) copy-start(bf16[144,288]{1,0:T(8,128)(2,1)} %param.26) | copy-start | bytes 248836
  7.2 185.3 %all-gather.19.cloned.1.call-start = ((), (), s32[]{:S(2)}) async-start(), calls=%async_computation.18 | async-start | bytes 2119680 | tf_op jit(solution)/shard_map/all_gather | solution.py:108
  53.2 6.7 copy-start.52
  54.6 106.0 %copy-start.92 = (bf16[288]{0:T(512)(128)(2,1)S(1)}, bf16[288]{0:T(512)(128)(2,1)}, u32[]{:S(2)}) copy-start(bf16[288]{0:T(512)(128)(2,1)} %param.27) | copy-start | bytes 1732
  54.6 106.0 %copy-start.57 = (bf16[288,144]{0,1:T(8,128)(2,1)S(1)}, bf16[288,144]{0,1:T(8,128)(2,1)}, u32[]{:S(2)}) copy-start(bf16[288,144]{0,1:T(8,128)(2,1)} %param.28) | copy-start | bytes 248836
  59.2 151.7 %all-gather.11.cloned.1.call-start = ((), (), s32[]{:S(2)}) async-start(), calls=%async_computation.14 | async-start | bytes 2119680 | tf_op jit(solution)/shard_map/all_gather | solution.py:108
  60.0 187.0 %reduce-scatter.47.cloned.1.call-start = ((), (), s32[]{:S(2)}) async-start(), calls=%async_computation.32 | async-start | bytes 4239360
  124.7 86.1 %copy-start.11 = (bf16[1152,288]{1,0:T(8,128)(2,1)}, bf16[1152,288]{1,0:T(8,128)(2,1)S(1)}, u32[]{:S(2)}) copy-start(bf16[1152,288]{1,0:T(8,128)(2,1)S(1)} %all_gather.45) | copy-start | bytes 1990660
  126.1 75.3 %copy-start.65 = (pred[736]{0:T(1024)(128)(4,1)}, pred[736]{0:T(1024)(128)(4,1)S(1)}, u32[]{:S(2)}) copy-start(pred[736]{0:T(1024)(128)(4,1)S(1)} %iota_compare_fusion) | copy-start | bytes 2212
  192.6 31.6 %copy-start.8 = (bf16[288,1152]{0,1:T(8,128)(2,1)}, bf16[288,1152]{0,1:T(8,128)(2,1)S(1)}, u32[]{:S(2)}) copy-start(bf16[288,1152]{0,1:T(8,128)(2,1)S(1)} %all_gather.46) | copy-start | bytes 1990660
  209.9 79.2 %reduce-scatter.43.cloned.1.call-start = ((), (), s32[]{:S(2)}) async-start(), calls=%async_computation.30 | async-start | bytes 4239360
  227.8 61.2 %copy-start.4 = (bf16[2,184,1152]{2,1,0:T(8,128)(2,1)S(1)}, bf16[2,184,1152]{2,1,0:T(8,128)(2,1)}, u32[]{:S(2)}) copy-start(bf16[2,184,1152]{2,1,0:T(8,128)(2,1)} %param.18) | copy-start | bytes 2543620
  227.8 83.6 %all-gather.23.cloned.1.call-start = ((), (), s32[]{:S(2)}) async-start(), calls=%async_computation.20 | async-start | bytes 2119680 | tf_op jit(solution)/shard_map/all_gather | solution.py:194
  230.5 138.0 %all-gather.17.cloned.1.call-start = ((), (), s32[]{:S(2)}) async-start(), calls=%async_computation.17 | async-start | bytes 2985984 | tf_op jit(solution)/shard_map/all_gather | solution.py:87
  231.1 193.2 %all-gather.15.cloned.1.call-start = ((), (), s32[]{:S(2)}) async-start(), calls=%async_computation.16 | async-start | bytes 2985984 | tf_op jit(solution)/shard_map/all_gather | solution.py:86
  231.8 213.0 %all-gather.13.cloned.1.call-start = ((), (), s32[]{:S(2)}) async-start(), calls=%async_computation.15 | async-start | bytes 2119680 | tf_op jit(solution)/shard_map/all_gather | solution.py:129
  292.6 174.2 %all-gather.27.cloned.1.call-start = ((), (), s32[]{:S(2)}) async-start(), calls=%async_computation.22 | async-start | bytes 2119680 | tf_op jit(solution)/shard_map/all_gather | solution.py:194
  293.3 195.2 %all-gather.21.cloned.1.call-start = ((), (), s32[]{:S(2)}) async-start(), calls=%async_computation.19 | async-start | bytes 2119680 | tf_op jit(solution)/shard_map/all_gather | solution.py:129
  293.9 236.7 %reduce-scatter.51.cloned.1.call-start = ((), (), s32[]{:S(2)}) async-start(), calls=%async_computation.34 | async-start | bytes 4239360
  444.8 11.4 copy-start.93
  460.8 111.9 %reduce-scatter.55.cloned.1.call-start = ((), (), s32[]{:S(2)}) async-start(), calls=%async_computation.36 | async-start | bytes 4239360
  488.5 11.4 copy-start.94
  504.3 110.3 %reduce-scatter.45.cloned.1.call-start = ((), (), s32[]{:S(2)}) async-start(), calls=%async_computation.31 | async-start | bytes 4239360
  512.4 144.3 %reduce-scatter.49.cloned.1.call-start = ((), (), s32[]{:S(2)}) async-start(), calls=%async_computation.33 | async-start | bytes 4239360
  520.1 164.7 %all-gather.29.cloned.1.call-start = ((), (), s32[]{:S(2)}) async-start(), calls=%async_computation.23 | async-start | bytes 2119680 | tf_op jit(solution)/shard_map/all_gather | solution.py:213
  574.7 86.5 %copy-start.72 = (f32[184]{0:T(256)S(1)}, f32[184]{0:T(256)}, u32[]{:S(2)}) copy-start(f32[184]{0:T(256)} %copy-done.71) | copy-start | bytes 2212
  574.7 86.5 %copy-start.75 = (f32[184]{0:T(256)S(1)}, f32[184]{0:T(256)}, u32[]{:S(2)}) copy-start(f32[184]{0:T(256)} %copy-done.74) | copy-start | bytes 2212
  660.3 24.6 %copy-start.9 = (bf16[288,1152]{0,1:T(8,128)(2,1)S(1)}, bf16[288,1152]{0,1:T(8,128)(2,1)}, u32[]{:S(2)}) copy-start(bf16[288,1152]{0,1:T(8,128)(2,1)} %copy-done.8) | copy-start | bytes 1990660
  660.3 26.8 %copy-start.79 = (f32[184]{0:T(256)}, f32[184]{0:T(256)S(1)}, u32[]{:S(2)}) copy-start(f32[184]{0:T(256)S(1)} %negate_multiply_fusion.1) | copy-start | bytes 2212
  660.3 26.8 %copy-start.80 = (f32[184]{0:T(256)}, f32[184]{0:T(256)S(1)}, u32[]{:S(2)}) copy-start(f32[184]{0:T(256)S(1)} %negate_multiply_fusion.3) | copy-start | bytes 2212
  664.4 45.6 %all-gather.25.cloned.1.call-start = ((), (), s32[]{:S(2)}) async-start(), calls=%async_computation.21 | async-start | bytes 2119680 | tf_op jit(solution)/shard_map/all_gather | solution.py:213
  665.0 117.2 %reduce-scatter.57.cloned.1.call-start = ((), (), s32[]{:S(2)}) async-start(), calls=%async_computation.37 | async-start | bytes 4239360
  687.2 6.8 slice-start.5
  687.2 14.6 %slice-start.8 = ((s8[4521984]{0:T(1024)(128)(4,1)}), s8[4194304]{0:T(1024)(128)(4,1)S(1)}, s32[]{:S(2)}) async-start(s8[4521984]{0:T(1024)(128)(4,1)} %bitcast.248), calls=%async_computation.46 | async-start | bytes 8388608
  693.9 7.9 slice-start.9
  709.8 81.7 %reduce-scatter.53.cloned.1.call-start = ((), (), s32[]{:S(2)}) async-start(), calls=%async_computation.35 | async-start | bytes 4239360
  713.2 6.7 copy-start.39
  713.2 6.7 slice-start
  713.2 8.0 slice-start.1
  713.2 8.1 slice-start.2
  713.2 14.2 %slice-start.6 = ((s8[4521984]{0:T(1024)(128)(4,1)}), s8[4194304]{0:T(1024)(128)(4,1)S(1)}, s32[]{:S(2)}) async-start(s8[4521984]{0:T(1024)(128)(4,1)} %bitcast.246), calls=%async_computation.44 | async-start | bytes 8388608
  734.7 166.2 %reduce-scatter.39.cloned.1.call-start = ((), (), s32[]{:S(2)}) async-start(), calls=%async_computation.28 | async-start | bytes 5971968 | tf_op jit(solution)/shard_map/reduce_scatter | solution.py:332
  745.5 263.9 %reduce-scatter.41.cloned.1.call-start = ((), (), s32[]{:S(2)}) async-start(), calls=%async_computation.29 | async-start | bytes 5971968 | tf_op jit(solution)/shard_map/reduce_scatter | solution.py:333
  756.8 322.4 %reduce-scatter.37.cloned.1.call-start = ((), (), s32[]{:S(2)}) async-start(), calls=%async_computation.27 | async-start | bytes 1990656 | tf_op jit(solution)/shard_map/reduce_scatter | solution.py:331
  763.1 385.7 %reduce-scatter.35.cloned.1.call-start = ((), (), s32[]{:S(2)}) async-start(), calls=%async_computation.26 | async-start | bytes 1990656 | tf_op jit(solution)/shard_map/reduce_scatter | solution.py:330
  768.3 449.4 %reduce-scatter.33.cloned.1.call-start = ((), (), s32[]{:S(2)}) async-start(), calls=%async_computation.25 | async-start | bytes 1990656 | tf_op jit(solution)/shard_map/reduce_scatter | solution.py:329
  773.5 513.2 %reduce-scatter.31.cloned.1.call-start = ((), (), s32[]{:S(2)}) async-start(), calls=%async_computation.24 | async-start | bytes 1990656 | tf_op jit(solution)/shard_map/reduce_scatter | solution.py:328
  779.4 12.0 copy-start.5
  779.4 12.0 copy-start.53
  779.5 12.0 copy-start.59
  779.5 12.0 copy-start.61
  781.9 11.6 copy-start.84
  781.9 11.6 copy-start.82
  781.9 11.7 copy-start.68
  781.9 11.7 copy-start.70
  781.9 14.6 %copy-start.66 = (f32[1,1152]{1,0:T(1,128)S(1)}, f32[1,1152]{1,0:T(1,128)}, u32[]{:S(2)}) copy-start(f32[1,1152]{1,0:T(1,128)} %add.515) | copy-start | bytes 13828
  791.5 53.0 %copy-start.19 = (f32[184,1152]{1,0:T(8,128)S(1)}, f32[184,1152]{1,0:T(8,128)}, u32[]{:S(2)}) copy-start(f32[184,1152]{1,0:T(8,128)} %reduce-scatter.53.cloned.1.call-done) | copy-start | bytes 2543620
  793.5 52.7 %copy-start.18 = (f32[184,1152]{1,0:T(8,128)S(1)}, f32[184,1152]{1,0:T(8,128)}, u32[]{:S(2)}) copy-start(f32[184,1152]{1,0:T(8,128)} %reduce-scatter.57.cloned.1.call-done) | copy-start | bytes 2543620
  793.5 52.7 %copy-start.73 = (f32[184]{0:T(256)S(1)}, f32[184]{0:T(256)}, u32[]{:S(2)}) copy-start(f32[184]{0:T(256)} %copy-done.71) | copy-start | bytes 2212
  796.4 49.8 %copy-start.77 = (f32[184]{0:T(256)S(1)}, f32[184]{0:T(256)}, u32[]{:S(2)}) copy-start(f32[184]{0:T(256)} %copy-done.76) | copy-start | bytes 2212
  (74 other events, 208.3 us)
Sparse Core Ops, SparseCore 0:
  59.3 17.5 all-gather.18
  79.0 20.3 all-gather.10
  210.0 36.9 reduce-scatter.46
  249.5 39.4 reduce-scatter.42
  291.0 20.3 all-gather.22
  313.4 55.0 all-gather.16
  370.6 53.5 all-gather.14
  425.8 18.9 all-gather.12
  446.4 20.3 all-gather.26
  468.1 20.3 all-gather.20
  491.1 39.4 reduce-scatter.50
  533.1 39.4 reduce-scatter.54
  575.2 39.4 reduce-scatter.44
  617.2 39.4 reduce-scatter.48
  664.5 20.3 all-gather.28
  686.3 20.3 all-gather.24
  709.9 39.4 reduce-scatter.56
  752.0 39.4 reduce-scatter.52
  795.6 105.2 reduce-scatter.38
  905.4 103.9 reduce-scatter.40
  1013.4 65.7 reduce-scatter.36
  1083.7 64.9 reduce-scatter.34
  1152.8 64.8 reduce-scatter.32
  1222.0 64.6 reduce-scatter.30
where the time goes:
time: 1300 us; the launch traced here: 1290 us
  waiting for transfers between devices  827 us (64%)
  blocking collectives  214 us (16%)
  matrix products  156 us (12%)
  other arithmetic  50 us (4%)
  local copies, waits for them, and re-layouts  26.7 us (2%)
  between operations  17.3 us (1%)
    unnamed x32, waiting for transfers between devices  205 us
    reduce_scatter x1, waiting for transfers between devices, local(): lax.psum_scatter(grad_w_down, 'fsdp', scatter_dimension=1, tiled=True)  108 us
    reduce_scatter x1, waiting for transfers between devices, local(): lax.psum_scatter(grad_w_out, 'fsdp', scatter_dimension=1, tiled=True)  69.9 us
    reduce_scatter x1, waiting for transfers between devices, local(): lax.psum_scatter(grad_wv, 'fsdp', scatter_dimension=0, tiled=True)  69.5 us
    reduce_scatter x1, waiting for transfers between devices, local(): lax.psum_scatter(grad_wq, 'fsdp', scatter_dimension=0, tiled=True)  69 us
    reduce_scatter x1, waiting for transfers between devices, local(): lax.psum_scatter(grad_wk, 'fsdp', scatter_dimension=0, tiled=True)  69 us
    all_gather x1, waiting for transfers between devices, fetch_weights(): lax.all_gather(down_weight, 'fsdp', axis=1, tiled=True)  57.1 us
    reduce_scatter x1, waiting for transfers between devices, local(): lax.psum_scatter(grad_w_up, 'fsdp', scatter_dimension=0, tiled=True)  52.2 us
  transfers between devices with their start and end apart: 24, of which 20 were waited for; matrix products, arithmetic and copies ran while one was open for 15% of the time, Pallas kernels for 0%

commit v1 on v0

--- a/solution.py
+++ b/solution.py
@@ -6,6 +6,27 @@
 HD = 72
 epsilon = 1e-06
 negative_big = -1e30
+
+
+def joined_along(blocks, dim):
+    blocks = jnp.moveaxis(blocks, 0, dim)
+    dims = blocks.shape
+    return blocks.reshape(*dims[:dim], dims[dim] * dims[dim + 1], *dims[dim + 2 :])
+
+
+def grow_blocks(x, axis):
+    size, mine = (lax.axis_size(axis), lax.axis_index(axis))
+    tiles, bit = (x[None], 1)
+    while bit < size:
+        other = lax.ppermute(tiles, axis, [(i, i ^ bit) for i in range(size)])
+        low = mine & bit == 0
+        tiles = jnp.concatenate([jnp.where(low, tiles, other), jnp.where(low, other, tiles)])
+        bit *= 2
+    return tiles
+
+
+def gather_by_bits(shard, axis, dim):
+    return joined_along(grow_blocks(shard, axis), dim)
 
 
 def layer_norm(row_block, gain_vec, shift_vec):
@@ -74,7 +95,7 @@
         attn_full = (
             lax.all_gather(ln1_gain, "fsdp", axis=0, tiled=True),
             lax.all_gather(ln1_bias, "fsdp", axis=0, tiled=True),
-            lax.all_gather(q_weight, "fsdp", axis=0, tiled=True),
+            gather_by_bits(q_weight, "fsdp", 0),
             lax.all_gather(k_weight, "fsdp", axis=0, tiled=True),
             lax.all_gather(v_weight, "fsdp", axis=0, tiled=True),
             lax.all_gather(out_weight, "fsdp", axis=1, tiled=True),

time: 1300 us -> 1270 us (0.977)
  blocking collectives: 214 us -> 185 us
    all_gather x1 -> x0, blocking collectives: 32.5 us -> none  [fetch_weights(): lax.all_gather(q_weight, 'fsdp', axis=0, tiled=True)]
  transfers between devices with their start and end apart: 24 -> 27, of which waited for: 20 -> 20; matrix products, arithmetic and copies ran while one was open for 15% -> 16% of each run, Pallas kernels for 0% -> 0%
where the time goes in v1:
time: 1270 us
  waiting for transfers between devices  833 us (66%)
  blocking collectives  185 us (15%)
  matrix products  154 us (12%)
  other arithmetic  50.7 us (4%)
  local copies, waits for them, and re-layouts  25.2 us (2%)
  between operations  17.2 us (1%)
    unnamed x32, waiting for transfers between devices  209 us
    reduce_scatter x1, waiting for transfers between devices, local(): lax.psum_scatter(grad_w_down, 'fsdp', scatter_dimension=1, tiled=True)  108 us
    reduce_scatter x1, waiting for transfers between devices, local(): lax.psum_scatter(grad_w_out, 'fsdp', scatter_dimension=1, tiled=True)  69.8 us
    reduce_scatter x1, waiting for transfers between devices, local(): lax.psum_scatter(grad_wv, 'fsdp', scatter_dimension=0, tiled=True)  69.6 us
    reduce_scatter x1, waiting for transfers between devices, local(): lax.psum_scatter(grad_wq, 'fsdp', scatter_dimension=0, tiled=True)  69.5 us
    reduce_scatter x1, waiting for transfers between devices, local(): lax.psum_scatter(grad_wk, 'fsdp', scatter_dimension=0, tiled=True)  68.8 us
    all_gather x1, waiting for transfers between devices, fetch_weights(): lax.all_gather(down_weight, 'fsdp', axis=1, tiled=True)  57.1 us
    reduce_scatter x1, waiting for transfers between devices, local(): lax.psum_scatter(grad_w_up, 'fsdp', scatter_dimension=0, tiled=True)  52.9 us
  transfers between devices with their start and end apart: 27, of which 20 were waited for; matrix products, arithmetic and copies ran while one was open for 16% of the time, Pallas kernels for 0%

profile of v1, /device:TPU:0, one launch (start us, length us, event | category | flops | bytes accessed | tf_op | source)
XLA Modules:
  0.0 1268.0 jit_solution(742294355445181545)
XLA Ops:
  14.3 39.4 %all-reduce.15 = (bf16[1152]{0:T(1024)(128)(2,1)S(1)}, bf16[1152]{0:T(1024)(128)(2,1)S(1)}, bf16[1152]{0:T(1024)(128)(2,1)}, bf16[1152]{0:T(1024)(128)(2,1)}, bf...) all-reduce(bf16[1152]{0:T(1024)(128)(2,1)S(1)} %dynamic-update-slice.1, ...), channel_id=1, replica_groups=mesh['fsdp'=8,'tp'=4] {'fsdp'}, use_global_device_ids=true, to_apply=%add.1 | all-reduce | flops 6912 | bytes 27648
  57.3 2.4 fusion.46
  60.6 32.9 %all_gather.42 = bf16[1152,288]{1,0:T(8,128)(2,1)S(1)} all-gather(bf16[144,288]{1,0:T(8,128)(2,1)S(1)} %copy-done.56), channel_id=1, replica_groups=mesh['fsdp'=8,'tp'=4] {'fsdp'}, dimensions={0}, use_global_device_ids=true | all-gather | bytes 746496 | tf_op jit(solution)/shard_map/all_gather | solution.py:99
  93.7 32.7 %all_gather.41 = bf16[1152,288]{1,0:T(8,128)(2,1)S(1)} all-gather(bf16[144,288]{1,0:T(8,128)(2,1)S(1)} %copy-done.57), channel_id=1, replica_groups=mesh['fsdp'=8,'tp'=4] {'fsdp'}, dimensions={0}, use_global_device_ids=true | all-gather | bytes 746496 | tf_op jit(solution)/shard_map/all_gather | solution.py:100
  128.7 35.9 %all_gather.43 = bf16[288,1152]{0,1:T(8,128)(2,1)S(1)} all-gather(bf16[288,144]{0,1:T(8,128)(2,1)S(1)} %copy-done.58), channel_id=1, replica_groups=mesh['fsdp'=8,'tp'=4] {'fsdp'}, dimensions={1}, use_global_device_ids=true | all-gather | bytes 746496 | tf_op jit(solution)/shard_map/all_gather | solution.py:101
  167.3 2.4 convolution_convert_fusion.6
  172.7 2.3 exponential_reduce_fusion
  180.6 3.0 fusion.86
  184.6 2.4 convolution_convert_fusion.7
  187.0 2.4 fusion.19
  191.6 2.3 exponential_reduce_fusion.1
  195.1 2.2 fusion.2
  199.5 2.9 fusion.85
  206.5 15.7 %reduce-scatter.47.cloned.1.call-done = f32[184,1152]{1,0:T(8,128)} async-done(((f32[736,1152]{1,0:T(8,128)}), f32[184,1152]{1,0:T(8,128)}) %reduce-scatter.47.cloned.1.call-update) | async-done | bytes 847888
  222.2 42.1 %reduce-scatter.43.cloned.1.call-done = f32[184,1152]{1,0:T(8,128)} async-done(((f32[736,1152]{1,0:T(8,128)}), f32[184,1152]{1,0:T(8,128)}) %reduce-scatter.43.cloned.1.call-update) | async-done | bytes 847888
  269.7 16.9 %all-gather.23.cloned.1.call-done = bf16[736,1152]{1,0:T(8,128)(2,1)} async-done(((bf16[184,1152]{1,0:T(8,128)(2,1)}), bf16[736,1152]{1,0:T(8,128)(2,1)}) %all-gather.23.cloned.1.call-update) | async-done | bytes 1695760 | tf_op jit(solution)/shard_map/all_gather | solution.py:215
  286.6 57.1 %all-gather.17.cloned.1.call-done = bf16[1076,1152]{0,1:T(8,128)(2,1)} async-done(((bf16[1076,144]{0,1:T(8,128)(2,1)}), bf16[1076,1152]{0,1:T(8,128)(2,1)}) %all-gather.17.cloned.1.call-update) | async-done | bytes 2479120 | tf_op jit(solution)/shard_map/all_gather | solution.py:108
  343.7 6.5 fusion.87
  350.2 49.4 %all-gather.15.cloned.1.call-done = bf16[1152,1076]{1,0:T(8,128)(2,1)} async-done(((bf16[144,1076]{1,0:T(8,128)(2,1)}), bf16[1152,1076]{1,0:T(8,128)(2,1)}) %all-gather.15.cloned.1.call-update) | async-done | bytes 2479120 | tf_op jit(solution)/shard_map/all_gather | solution.py:107
  399.5 20.5 %all-gather.13.cloned.1.call-done = bf16[736,1152]{1,0:T(8,128)(2,1)} async-done(((bf16[184,1152]{1,0:T(8,128)(2,1)}), bf16[736,1152]{1,0:T(8,128)(2,1)}) %all-gather.13.cloned.1.call-update) | async-done | bytes 1695760 | tf_op jit(solution)/shard_map/all_gather | solution.py:150
  420.1 10.3 convert_reduce_fusion.1
  431.5 4.6 fusion.88
  436.3 5.7 all-gather.27.cloned.1.call-done
  442.0 6.4 fusion.90
  448.4 15.4 %all-gather.21.cloned.1.call-done = bf16[736,1152]{1,0:T(8,128)(2,1)} async-done(((bf16[184,1152]{1,0:T(8,128)(2,1)}), bf16[736,1152]{1,0:T(8,128)(2,1)}) %all-gather.21.cloned.1.call-update) | async-done | bytes 1695760 | tf_op jit(solution)/shard_map/all_gather | solution.py:150
  463.8 10.2 convert_reduce_fusion
  475.1 4.4 fusion.91
  479.9 7.8 fusion.73
  487.7 7.6 fusion.74
  495.5 10.4 reduce-scatter.51.cloned.1.call-done
  505.8 42.1 %reduce-scatter.55.cloned.1.call-done = f32[184,1152]{1,0:T(8,128)} async-done(((f32[736,1152]{1,0:T(8,128)}), f32[184,1152]{1,0:T(8,128)}) %reduce-scatter.55.cloned.1.call-update) | async-done | bytes 847888
  550.0 39.9 %reduce-scatter.45.cloned.1.call-done = f32[184,1152]{1,0:T(8,128)} async-done(((f32[736,1152]{1,0:T(8,128)}), f32[184,1152]{1,0:T(8,128)}) %reduce-scatter.45.cloned.1.call-update) | async-done | bytes 847888
  589.9 42.1 %reduce-scatter.49.cloned.1.call-done = f32[184,1152]{1,0:T(8,128)} async-done(((f32[736,1152]{1,0:T(8,128)}), f32[184,1152]{1,0:T(8,128)}) %reduce-scatter.49.cloned.1.call-update) | async-done | bytes 847888
  632.0 3.5 fusion.78
  636.5 2.5 fusion.54
  640.0 19.5 %all-gather.29.cloned.1.call-done = bf16[736,1152]{1,0:T(8,128)(2,1)} async-done(((bf16[184,1152]{1,0:T(8,128)(2,1)}), bf16[736,1152]{1,0:T(8,128)(2,1)}) %all-gather.29.cloned.1.call-update) | async-done | bytes 1695760 | tf_op jit(solution)/shard_map/all_gather | solution.py:234
  659.5 2.2 convolution_convert_fusion.4
  661.8 6.1 multiply_reduce_fusion
  668.6 2.8 multiply_convert_fusion
  678.2 3.0 convolution_add_fusion.2
  684.7 6.0 multiply_reduce_fusion.1
  691.8 2.8 multiply_convert_fusion.1
  702.2 2.9 convolution_add_fusion.4
  706.5 4.2 fusion.97
  710.7 5.1 convolution_add_fusion.1
  717.3 4.8 fusion.72
  722.1 5.1 convolution_add_fusion
  728.2 2.7 fusion.96
  731.0 2.5 convolution_add_fusion.8
  733.5 3.1 fusion.95
  736.6 2.4 convolution_add_fusion.9
  739.1 2.6 fusion.94
  741.8 2.4 convolution_add_fusion.10
  746.7 2.6 fusion.93
  749.4 2.4 convolution_add_fusion.11
  752.1 13.2 %reduce-scatter.53.cloned.1.call-done = f32[184,1152]{1,0:T(8,128)} async-done(((f32[736,1152]{1,0:T(8,128)}), f32[184,1152]{1,0:T(8,128)}) %reduce-scatter.53.cloned.1.call-update) | async-done | bytes 847888
  767.4 2.9 fusion.47
  770.3 43.7 %all-reduce.14 = (f32[6,1152]{1,0:T(8,128)}, f32[2,1152]{1,0:T(2,128)S(1)}, f32[4304]{0:T(1024)S(1)}) all-reduce(f32[6,1152]{1,0:T(8,128)S(1)} %stack.38, f32[2,1152]{1,0:T(2,128)S(1)} %dynamic_update_slice.6, f32[4304]{0:T(1024)S(1)} %add_dynamic-update-slice_fusion), channel_id=1, replica_groups=mesh['fsdp'=8,'tp'=4] {'fsdp','tp'}, use_global_device_ids=true, to_apply=%region_42.43 | all-reduce | flops 13520 | bytes 108160 | tf_op jit(solution)/shard_map/psum | solution.py:365
  821.8 52.9 %reduce-scatter.39.cloned.1.call-done = f32[144,1076]{1,0:T(8,128)} async-done(((f32[1152,1076]{1,0:T(8,128)}), f32[144,1076]{1,0:T(8,128)}) %reduce-scatter.39.cloned.1.call-update) | async-done | bytes 619792 | tf_op jit(solution)/shard_map/reduce_scatter | solution.py:353
  874.6 108.4 %reduce-scatter.41.cloned.1.call-done = f32[1076,144]{0,1:T(8,128)} async-done(((f32[1076,1152]{0,1:T(8,128)}), f32[1076,144]{0,1:T(8,128)}) %reduce-scatter.41.cloned.1.call-update) | async-done | bytes 619792 | tf_op jit(solution)/shard_map/reduce_scatter | solution.py:354
  983.0 69.8 %reduce-scatter.37.cloned.1.call-done = f32[288,144]{0,1:T(8,128)} async-done(((f32[288,1152]{0,1:T(8,128)}), f32[288,144]{0,1:T(8,128)}) %reduce-scatter.37.cloned.1.call-update) | async-done | bytes 165904 | tf_op jit(solution)/shard_map/reduce_scatter | solution.py:352
  1052.8 69.6 %reduce-scatter.35.cloned.1.call-done = f32[144,288]{1,0:T(8,128)} async-done(((f32[1152,288]{1,0:T(8,128)}), f32[144,288]{1,0:T(8,128)}) %reduce-scatter.35.cloned.1.call-update) | async-done | bytes 165904 | tf_op jit(solution)/shard_map/reduce_scatter | solution.py:351
  1122.4 68.8 %reduce-scatter.33.cloned.1.call-done = f32[144,288]{1,0:T(8,128)} async-done(((f32[1152,288]{1,0:T(8,128)}), f32[144,288]{1,0:T(8,128)}) %reduce-scatter.33.cloned.1.call-update) | async-done | bytes 165904 | tf_op jit(solution)/shard_map/reduce_scatter | solution.py:350
  1191.3 69.5 %reduce-scatter.31.cloned.1.call-done = f32[144,288]{1,0:T(8,128)} async-done(((f32[1152,288]{1,0:T(8,128)}), f32[144,288]{1,0:T(8,128)}) %reduce-scatter.31.cloned.1.call-update) | async-done | bytes 165904 | tf_op jit(solution)/shard_map/reduce_scatter | solution.py:349
  (372 shorter events, 82.7 us)
Async XLA Ops:
  7.2 52.6 %copy-start.55 = (bf16[144,288]{1,0:T(8,128)(2,1)S(1)}, bf16[144,288]{1,0:T(8,128)(2,1)}, u32[]{:S(2)}) copy-start(bf16[144,288]{1,0:T(8,128)(2,1)} %param.23) | copy-start | bytes 248836
  7.2 53.4 %copy-start.56 = (bf16[144,288]{1,0:T(8,128)(2,1)S(1)}, bf16[144,288]{1,0:T(8,128)(2,1)}, u32[]{:S(2)}) copy-start(bf16[144,288]{1,0:T(8,128)(2,1)} %param.25) | copy-start | bytes 248836
  7.2 86.5 %copy-start.57 = (bf16[144,288]{1,0:T(8,128)(2,1)S(1)}, bf16[144,288]{1,0:T(8,128)(2,1)}, u32[]{:S(2)}) copy-start(bf16[144,288]{1,0:T(8,128)(2,1)} %param.26) | copy-start | bytes 248836
  7.2 160.0 %all-gather.19.cloned.1.call-start = ((), (), s32[]{:S(2)}) async-start(), calls=%async_computation.18 | async-start | bytes 2119680 | tf_op jit(solution)/shard_map/all_gather | solution.py:129
  55.1 71.3 %copy-start.78 = (s32[2]{0:T(128)S(1)}, s32[2]{0:T(128)}, u32[]{:S(2)}) copy-start(s32[2]{0:T(128)} %param.20) | copy-start | bytes 28
  55.1 71.9 %copy-start.59 = (f32[184]{0:T(256)}, f32[184]{0:T(256)S(1)}, u32[]{:S(2)}) copy-start(f32[184]{0:T(256)S(1)} %get-tuple-element.118) | copy-start | bytes 2212
  55.1 71.9 %copy-start.61 = (f32[184]{0:T(256)}, f32[184]{0:T(256)S(1)}, u32[]{:S(2)}) copy-start(f32[184]{0:T(256)S(1)} %get-tuple-element.119) | copy-start | bytes 2212
  56.7 70.4 %copy-start.70 = (f32[184]{0:T(256)}, f32[184]{0:T(256)S(1)}, u32[]{:S(2)}) copy-start(f32[184]{0:T(256)S(1)} %get-tuple-element.40) | copy-start | bytes 2212
  57.2 69.8 %copy-start.65 = (f32[184]{0:T(256)}, f32[184]{0:T(256)S(1)}, u32[]{:S(2)}) copy-start(f32[184]{0:T(256)S(1)} %fusion.62) | copy-start | bytes 2212
  57.2 69.8 %copy-start.63 = (f32[184]{0:T(256)}, f32[184]{0:T(256)S(1)}, u32[]{:S(2)}) copy-start(f32[184]{0:T(256)S(1)} %fusion.64) | copy-start | bytes 2212
  57.2 71.4 %copy-start.79 = (bf16[288]{0:T(512)(128)(2,1)S(1)}, bf16[288]{0:T(512)(128)(2,1)}, u32[]{:S(2)}) copy-start(bf16[288]{0:T(512)(128)(2,1)} %param.24) | copy-start | bytes 1732
  57.3 71.5 %copy-start.80 = (bf16[288]{0:T(512)(128)(2,1)S(1)}, bf16[288]{0:T(512)(128)(2,1)}, u32[]{:S(2)}) copy-start(bf16[288]{0:T(512)(128)(2,1)} %param.27) | copy-start | bytes 1732
  57.3 71.5 %copy-start.58 = (bf16[288,144]{0,1:T(8,128)(2,1)S(1)}, bf16[288,144]{0,1:T(8,128)(2,1)}, u32[]{:S(2)}) copy-start(bf16[288,144]{0,1:T(8,128)(2,1)} %param.28) | copy-start | bytes 248836
  59.7 124.9 %all-gather.11.cloned.1.call-start = ((), (), s32[]{:S(2)}) async-start(), calls=%async_computation.14 | async-start | bytes 2119680 | tf_op jit(solution)/shard_map/all_gather | solution.py:129
  59.8 33.7 %collective-permute-start = (bf16[1,144,288]{2,1,0:T(8,128)(2,1)S(1)}, bf16[1,144,288]{2,1,0:T(8,128)(2,1)S(1)}, u32[]{:S(2)}, u32[]{:S(2)}) collective-permute-start(bf16[1,144,288]{2,1,0:T(8,128)(2,1)S(1)} %bitcast.290), channel_id=1, source_target_pairs={{0,4},{4,0},{8,12},{12,8},{16,20},{20,16},{24,28},{28,24},{1,5},{5... | collective-permute-start | bytes 248840 | tf_op jit(solution)/shard_map/ppermute | solution.py:21
  60.5 161.7 %reduce-scatter.47.cloned.1.call-start = ((), (), s32[]{:S(2)}) async-start(), calls=%async_computation.32 | async-start | bytes 4239360
  93.6 33.5 %collective-permute-start.1 = (bf16[2,144,288]{2,1,0:T(8,128)(2,1)S(1)}, bf16[2,144,288]{2,1,0:T(8,128)(2,1)S(1)}, u32[]{:S(2)}, u32[]{:S(2)}) collective-permute-start(bf16[2,144,288]{2,1,0:T(8,128)(2,1)S(1)} %pad_maximum_fusion.4), channel_id=1, source_target_pairs={{0,8},{4,12},{8,0},{12,4},{16,24},{20,28},{24,16},{28,20},{1,9},{5... | collective-permute-start | bytes 497672 | tf_op jit(solution)/shard_map/ppermute | solution.py:21
  126.4 67.5 %copy-start.11 = (bf16[1152,288]{1,0:T(8,128)(2,1)}, bf16[1152,288]{1,0:T(8,128)(2,1)S(1)}, u32[]{:S(2)}) copy-start(bf16[1152,288]{1,0:T(8,128)(2,1)S(1)} %all_gather.41) | copy-start | bytes 1990660
  128.0 36.7 %collective-permute-start.2 = (bf16[4,144,288]{2,1,0:T(8,128)(2,1)}, bf16[4,144,288]{2,1,0:T(8,128)(2,1)}, u32[]{:S(2)}, u32[]{:S(2)}) collective-permute-start(bf16[4,144,288]{2,1,0:T(8,128)(2,1)} %pad_maximum_fusion.3), channel_id=1, source_target_pairs={{0,16},{4,20},{8,24},{12,28},{16,0},{20,4},{24,8},{28,12},{1,17},{... | collective-permute-start | bytes 995336 | tf_op jit(solution)/shard_map/ppermute | solution.py:21
  164.7 34.8 %copy-start.8 = (bf16[288,1152]{0,1:T(8,128)(2,1)}, bf16[288,1152]{0,1:T(8,128)(2,1)S(1)}, u32[]{:S(2)}) copy-start(bf16[288,1152]{0,1:T(8,128)(2,1)S(1)} %all_gather.43) | copy-start | bytes 1990660
  183.6 80.7 %reduce-scatter.43.cloned.1.call-start = ((), (), s32[]{:S(2)}) async-start(), calls=%async_computation.30 | async-start | bytes 4239360
  202.4 61.9 %copy-start.4 = (bf16[2,184,1152]{2,1,0:T(8,128)(2,1)S(1)}, bf16[2,184,1152]{2,1,0:T(8,128)(2,1)}, u32[]{:S(2)}) copy-start(bf16[2,184,1152]{2,1,0:T(8,128)(2,1)} %param.18) | copy-start | bytes 2543620
  202.4 84.2 %all-gather.23.cloned.1.call-start = ((), (), s32[]{:S(2)}) async-start(), calls=%async_computation.20 | async-start | bytes 2119680 | tf_op jit(solution)/shard_map/all_gather | solution.py:215
  205.0 138.7 %all-gather.17.cloned.1.call-start = ((), (), s32[]{:S(2)}) async-start(), calls=%async_computation.17 | async-start | bytes 2985984 | tf_op jit(solution)/shard_map/all_gather | solution.py:108
  205.6 193.9 %all-gather.15.cloned.1.call-start = ((), (), s32[]{:S(2)}) async-start(), calls=%async_computation.16 | async-start | bytes 2985984 | tf_op jit(solution)/shard_map/all_gather | solution.py:107
  206.4 213.7 %all-gather.13.cloned.1.call-start = ((), (), s32[]{:S(2)}) async-start(), calls=%async_computation.15 | async-start | bytes 2119680 | tf_op jit(solution)/shard_map/all_gather | solution.py:150
  267.9 174.1 %all-gather.27.cloned.1.call-start = ((), (), s32[]{:S(2)}) async-start(), calls=%async_computation.22 | async-start | bytes 2119680 | tf_op jit(solution)/shard_map/all_gather | solution.py:215
  268.6 195.2 %all-gather.21.cloned.1.call-start = ((), (), s32[]{:S(2)}) async-start(), calls=%async_computation.19 | async-start | bytes 2119680 | tf_op jit(solution)/shard_map/all_gather | solution.py:150
  269.2 236.7 %reduce-scatter.51.cloned.1.call-start = ((), (), s32[]{:S(2)}) async-start(), calls=%async_computation.34 | async-start | bytes 4239360
  420.1 11.5 copy-start.81
  436.1 111.8 %reduce-scatter.55.cloned.1.call-start = ((), (), s32[]{:S(2)}) async-start(), calls=%async_computation.36 | async-start | bytes 4239360
  463.8 11.3 copy-start.82
  479.6 110.3 %reduce-scatter.45.cloned.1.call-start = ((), (), s32[]{:S(2)}) async-start(), calls=%async_computation.31 | async-start | bytes 4239360
  487.7 144.3 %reduce-scatter.49.cloned.1.call-start = ((), (), s32[]{:S(2)}) async-start(), calls=%async_computation.33 | async-start | bytes 4239360
  495.4 164.1 %all-gather.29.cloned.1.call-start = ((), (), s32[]{:S(2)}) async-start(), calls=%async_computation.23 | async-start | bytes 2119680 | tf_op jit(solution)/shard_map/all_gather | solution.py:234
  635.5 26.2 %copy-start.19 = (f32[184,1152]{1,0:T(8,128)}, f32[184,1152]{1,0:T(8,128)S(1)}, u32[]{:S(2)}) copy-start(f32[184,1152]{1,0:T(8,128)S(1)} %get-tuple-element.90) | copy-start | bytes 2543620
  635.5 24.0 %copy-start.9 = (bf16[288,1152]{0,1:T(8,128)(2,1)S(1)}, bf16[288,1152]{0,1:T(8,128)(2,1)}, u32[]{:S(2)}) copy-start(bf16[288,1152]{0,1:T(8,128)(2,1)} %copy-done.8) | copy-start | bytes 1990660
  635.5 26.2 %copy-start.67 = (f32[184]{0:T(256)}, f32[184]{0:T(256)S(1)}, u32[]{:S(2)}) copy-start(f32[184]{0:T(256)S(1)} %negate_multiply_fusion.3) | copy-start | bytes 2212
  639.0 42.5 %all-gather.25.cloned.1.call-start = ((), (), s32[]{:S(2)}) async-start(), calls=%async_computation.21 | async-start | bytes 2119680 | tf_op jit(solution)/shard_map/all_gather | solution.py:234
  639.6 112.5 %reduce-scatter.57.cloned.1.call-start = ((), (), s32[]{:S(2)}) async-start(), calls=%async_computation.37 | async-start | bytes 4239360
  661.8 6.6 slice-start.4
  661.8 6.7 slice-start.5
  661.8 12.2 slice-start.8
  681.2 84.0 %reduce-scatter.53.cloned.1.call-start = ((), (), s32[]{:S(2)}) async-start(), calls=%async_computation.35 | async-start | bytes 4239360
  684.7 6.9 slice-start.1
  684.7 7.1 slice-start.2
  684.7 13.4 %slice-start.6 = ((s8[4521984]{0:T(1024)(128)(4,1)}), s8[4194304]{0:T(1024)(128)(4,1)S(1)}, s32[]{:S(2)}) async-start(s8[4521984]{0:T(1024)(128)(4,1)} %bitcast.250), calls=%async_computation.44 | async-start | bytes 8388608
  705.1 169.5 %reduce-scatter.39.cloned.1.call-start = ((), (), s32[]{:S(2)}) async-start(), calls=%async_computation.28 | async-start | bytes 5971968 | tf_op jit(solution)/shard_map/reduce_scatter | solution.py:353
  715.8 267.2 %reduce-scatter.41.cloned.1.call-start = ((), (), s32[]{:S(2)}) async-start(), calls=%async_computation.29 | async-start | bytes 5971968 | tf_op jit(solution)/shard_map/reduce_scatter | solution.py:354
  727.2 325.6 %reduce-scatter.37.cloned.1.call-start = ((), (), s32[]{:S(2)}) async-start(), calls=%async_computation.27 | async-start | bytes 1990656 | tf_op jit(solution)/shard_map/reduce_scatter | solution.py:352
  733.5 388.9 %reduce-scatter.35.cloned.1.call-start = ((), (), s32[]{:S(2)}) async-start(), calls=%async_computation.26 | async-start | bytes 1990656 | tf_op jit(solution)/shard_map/reduce_scatter | solution.py:351
  739.1 452.2 %reduce-scatter.33.cloned.1.call-start = ((), (), s32[]{:S(2)}) async-start(), calls=%async_computation.25 | async-start | bytes 1990656 | tf_op jit(solution)/shard_map/reduce_scatter | solution.py:350
  744.2 516.5 %reduce-scatter.31.cloned.1.call-start = ((), (), s32[]{:S(2)}) async-start(), calls=%async_computation.24 | async-start | bytes 1990656 | tf_op jit(solution)/shard_map/reduce_scatter | solution.py:349
  749.4 15.9 %copy-start.5 = (bf16[2,184,1152]{2,1,0:T(8,128)(2,1)S(1)}, bf16[2,184,1152]{2,1,0:T(8,128)(2,1)}, u32[]{:S(2)}) copy-start(bf16[2,184,1152]{2,1,0:T(8,128)(2,1)} %param.18) | copy-start | bytes 2543620
  749.4 15.9 %copy-start.54 = (f32[1152]{0:T(1024)S(1)}, f32[1152]{0:T(1024)}, u32[]{:S(2)}) copy-start(f32[1152]{0:T(1024)} %copy-done.53) | copy-start | bytes 13828
  749.4 15.9 %copy-start.60 = (f32[184]{0:T(256)S(1)}, f32[184]{0:T(256)}, u32[]{:S(2)}) copy-start(f32[184]{0:T(256)} %copy-done.59) | copy-start | bytes 2212
  749.4 15.9 %copy-start.62 = (f32[184]{0:T(256)S(1)}, f32[184]{0:T(256)}, u32[]{:S(2)}) copy-start(f32[184]{0:T(256)} %copy-done.61) | copy-start | bytes 2212
  751.8 15.4 %copy-start.71 = (f32[184]{0:T(256)S(1)}, f32[184]{0:T(256)}, u32[]{:S(2)}) copy-start(f32[184]{0:T(256)} %copy-done.70) | copy-start | bytes 2212
  751.8 15.5 %copy-start.69 = (f32[184]{0:T(256)S(1)}, f32[184]{0:T(256)}, u32[]{:S(2)}) copy-start(f32[184]{0:T(256)} %copy-done.68) | copy-start | bytes 2212
  751.8 15.5 %copy-start.64 = (f32[184]{0:T(256)S(1)}, f32[184]{0:T(256)}, u32[]{:S(2)}) copy-start(f32[184]{0:T(256)} %copy-done.63) | copy-start | bytes 2212
  751.8 15.5 %copy-start.66 = (f32[184]{0:T(256)S(1)}, f32[184]{0:T(256)}, u32[]{:S(2)}) copy-start(f32[184]{0:T(256)} %copy-done.65) | copy-start | bytes 2212
  765.3 53.0 %copy-start.18 = (f32[184,1152]{1,0:T(8,128)S(1)}, f32[184,1152]{1,0:T(8,128)}, u32[]{:S(2)}) copy-start(f32[184,1152]{1,0:T(8,128)} %reduce-scatter.53.cloned.1.call-done) | copy-start | bytes 2543620
  767.2 52.7 %copy-start.17 = (f32[184,1152]{1,0:T(8,128)S(1)}, f32[184,1152]{1,0:T(8,128)}, u32[]{:S(2)}) copy-start(f32[184,1152]{1,0:T(8,128)} %reduce-scatter.57.cloned.1.call-done) | copy-start | bytes 2543620
  767.2 52.7 %copy-start.20 = (f32[184,1152]{1,0:T(8,128)S(1)}, f32[184,1152]{1,0:T(8,128)}, u32[]{:S(2)}) copy-start(f32[184,1152]{1,0:T(8,128)} %copy-done.19) | copy-start | bytes 2543620
  (65 other events, 187.3 us)
Sparse Core Ops, SparseCore 0:
  59.9 17.5 all-gather.18
  79.6 20.3 all-gather.10
  183.7 38.4 reduce-scatter.46
  224.8 39.4 reduce-scatter.42
  266.3 20.3 all-gather.22
  288.7 55.0 all-gather.16
  345.9 53.5 all-gather.14
  401.1 18.9 all-gather.12
  421.6 20.3 all-gather.26
  443.4 20.3 all-gather.20
  466.3 39.4 reduce-scatter.50
  508.4 39.4 reduce-scatter.54
  550.4 39.4 reduce-scatter.44
  592.5 39.4 reduce-scatter.48
  639.1 20.3 all-gather.28
  660.9 20.3 all-gather.24
  683.7 39.4 reduce-scatter.56
  725.8 39.4 reduce-scatter.52
  769.4 105.1 reduce-scatter.38
  879.1 103.9 reduce-scatter.40
  987.1 65.7 reduce-scatter.36
  1057.2 65.1 reduce-scatter.34
  1126.5 64.7 reduce-scatter.32
  1195.5 65.1 reduce-scatter.30
